TPU v7x, 256 devices: a whole 4x4x8 slice. The times are simulated.
256 devices in a mesh: group: 4 (over z_hi), member: 64 (over y, x, z_lo, core).
Axes of the slice: x: 4, y: 4, z: 8 (z_hi: 4, z_lo: 2; z = z_hi * 2 + z_lo), core: 2. Of those that a mesh axis runs over, the one named last changes fastest.
Arguments:
- audio_vectors: bfloat16 [32768, 768], P(('group', 'member')), may hold values from -8 to 8
- sentence_vectors: bfloat16 [16384, 768], P(('group', 'member')), may hold values from -8 to 8
- matching_indices: int32 [32768], P(('group', 'member')), may hold values from 0 to 16383, as said below
- sharpness_array: float32 [1], replicated, may hold values from 8 to 16
- offset_term: float32 [1], replicated, may hold values from -4 to -2
Outputs:
- speech_grad: float32 [32768, 768], P(('group', 'member'))
- text_grad: float32 [16384, 768], P(('group', 'member'))
Inputs may be any that keep to these rules, and one draw needn't show every extreme that they name: `matching_indices`: each caption matches exactly two speech clips.
All inputs are finite; a program needn't handle non-finite values.
Results may differ from a plain program's by a relative error of at most 0.00072.
Values may be sent and summed in bfloat16 or wider, within the bound.
A program may use at most 128 MiB of HBM per device.

v0:
```python
import jax
import jax.numpy as jnp
from jax import lax
from jax.sharding import Mesh
from jax.sharding import PartitionSpec as P

MEMBER = ("member_0", "member_1", "member_2", "member_3")
GROUP_MEMBER = ("group", "member_0", "member_1", "member_2", "member_3")


def joined_along(blocks, dim):
    blocks = jnp.moveaxis(blocks, 0, dim)
    lengths = blocks.shape
    return blocks.reshape(*lengths[:dim], lengths[dim] * lengths[dim + 1], *lengths[dim + 2 :])


def copy_for_each(value, axis):
    size = lax.axis_size(axis)
    return lax.all_to_all(
        jnp.broadcast_to(value[None], (size, *value.shape)), axis, 0, 0, tiled=True
    )


def gather_directly(value, axis, dim):
    return joined_along(copy_for_each(value, axis), dim)


def split_up(value, dim, size):
    before, after = (value.shape[:dim], value.shape[dim + 1 :])
    return jnp.moveaxis(value.reshape(*before, size, -1, *after), dim, 0)


def sum_at_owner(value, axis, dim):
    size = lax.axis_size(axis)
    blocks = lax.all_to_all(split_up(value, dim, size), axis, 0, 0, tiled=True)
    return jnp.sum(blocks, axis=0)


def scatter_pairs(value, chips, core, dim):
    sizes = (lax.axis_size(chips), lax.axis_size(core))
    blocks = split_up(value, dim, sizes[0] * sizes[1])
    inside = blocks.shape[1:]
    blocks = blocks.reshape(*sizes, *inside).swapaxes(0, 1).reshape(-1, *inside)
    blocks = lax.psum_scatter(blocks, core, scatter_dimension=0, tiled=True)
    return lax.psum_scatter(blocks, chips, scatter_dimension=0, tiled=True)[0]


def unit_rows(values):
    floats = values.astype(jnp.float32)
    norms = jnp.sqrt(jnp.sum(floats * floats, axis=-1, keepdims=True) + 1e-06)
    return (floats / norms, norms)


def project_gradient(back, direction, norms):
    along = jnp.sum(direction * back, axis=-1, keepdims=True)
    return (back - direction * along) / norms


def pair_coef(audio_entries, label_rows, text_rows, columns, sharpness_factor, shift):
    logits = (
        sharpness_factor * jnp.dot(audio_entries, text_rows.T, preferred_element_type=jnp.float32)
        + shift
    )
    match = (label_rows[:, None] == columns[None, :]).astype(jnp.float32)
    return (sharpness_factor * (jax.nn.sigmoid(logits) - match)).astype(jnp.bfloat16)


def column_product(pair_weight, visitor):
    return lax.dot_general(
        pair_weight, visitor, (((0,), (0,)), ((), ())), preferred_element_type=jnp.float32
    )


def shards(audio_vectors, sentence_vectors, matching_indices, sharpness_array, offset_term):
    audio_heading, speech_norm = unit_rows(audio_vectors)
    text_dir, text_norm = unit_rows(sentence_vectors)
    speech_unit = audio_heading.astype(jnp.bfloat16)
    text_normalized = text_dir.astype(jnp.bfloat16)
    sharpness_factor = sharpness_array[0]
    shift = offset_term[0]
    group_now = lax.axis_index("group")
    text_rows = lax.all_gather(text_normalized, MEMBER, axis=0, tiled=True)
    width = text_rows.shape[0]
    columns = group_now * width + jnp.arange(width, dtype=jnp.int32)
    label_all = lax.all_gather(matching_indices, "group", axis=0, tiled=True)
    speech_all = gather_directly(speech_unit, "group", 0)
    pair_weight = pair_coef(speech_all, label_all, text_rows, columns, sharpness_factor, shift)
    speech_part = jnp.dot(pair_weight, text_rows, preferred_element_type=jnp.float32)
    speech_gradient_back = sum_at_owner(speech_part, "group", 0)
    text_part = column_product(pair_weight, speech_all)
    text_back = scatter_pairs(text_part, ("member_0", "member_1", "member_2"), "member_3", 0)
    speech_grad = project_gradient(speech_gradient_back, audio_heading, speech_norm)
    text_grad = project_gradient(text_back, text_dir, text_norm)
    return (speech_grad, text_grad)


def solution(mesh):
    split = Mesh(
        mesh.devices.reshape(mesh.shape["group"], 4, 4, 2, 2),
        ("group", "member_0", "member_1", "member_2", "member_3"),
    )
    return jax.shard_map(
        shards,
        mesh=split,
        in_specs=(P(GROUP_MEMBER, None), P(GROUP_MEMBER, None), P(GROUP_MEMBER), P(), P()),
        out_specs=(P(GROUP_MEMBER, None), P(GROUP_MEMBER, None)),
        check_vma=False,
    )
```

profile of v0, /device:TPU:64, one launch (start us, length us, event | category | flops | bytes accessed | tf_op | source)
XLA Modules:
  0.0 414.7 jit_solution(13824116031976714388)
XLA Ops:
  7.2 0.0 all-gather.3.cloned.1.call-start
  7.2 1.0 fusion.7
  8.2 1.6 fusion.10
  9.9 0.0 all-gather.3.cloned.1.call-update
  9.9 1.0 fusion.6
  11.0 1.0 fusion.11
  12.0 0.9 broadcast_in_dim.2
  12.9 8.1 %all-to-all-start = ((bf16[4,128,768]{2,1,0:T(8,128)(2,1)}), bf16[4,128,768]{2,1,0:T(8,128)(2,1)S(1)}, u32[]{:S(2)}, u32[]{:S(2)}) async-start(bf16[4,128,768]{2,1,0:T(8,128)(2,1)} %broadcast_in_dim.2), calls=%async_computation | async-start | bytes 1572864 | tf_op jit(solution)/shard_map/all_to_all | solution.py:19
  22.3 27.0 %all-gather = s32[4,1,128]{2,1,0:T(1,128)S(1)} all-gather(s32[1,1,128]{2,1,0:T(1,128)} %bitcast.42), channel_id=1, replica_groups=mesh['group'=4,'member_0'=4,'member_1'=4,'member_2'=2,'member_3'=2] {'gr..., dimensions={0}, use_global_device_ids=true | all-gather | bytes 2560 | tf_op jit(solution)/shard_map/all_gather | solution.py:85
  49.4 75.7 %all-gather.3.cloned.1.call-done = bf16[4096,768]{1,0:T(8,128)(2,1)} async-done(((bf16[64,768]{1,0:T(8,128)(2,1)}), bf16[4096,768]{1,0:T(8,128)(2,1)}) %all-gather.3.cloned.1.call-update) | async-done | bytes 6291472 | tf_op jit(solution)/shard_map/all_gather | solution.py:82
  125.0 10.1 %fusion.1 = (bf16[4096,512]{0,1:T(8,128)(2,1)}, f32[512,4096]{1,0:T(8,128)}) fusion(s32[4096]{0:T(1024)S(1)} %iota_add_fusion, f32[]{:T(128)} %bitcast.33, s32[512]{0:T(512)S(1)} %bitcast.40, f32[]{:T(128)} %bitcast.34, bf16[512,768]{1,0:T(8,128)(2,1)S(1)} %bitcast.38, bf16[4096,768]{1,0:T(8,128)(2,1)} %all-gather.3.cloned.1.call-done), kind=kOutput, calls=%fused_computation.2 | convolution fusion | flops 3242196992 | bytes 19679240 | tf_op jit(solution)/shard_map/dot_general | solution.py:61
  135.2 6.5 %copy.10 = bf16[4096,512]{1,0:T(8,128)(2,1)} copy(bf16[4096,512]{0,1:T(8,128)(2,1)} %get-tuple-element.2) | data formatting | bytes 8388608 | tf_op jit(solution)/shard_map/convert_element_type | solution.py:65
  141.7 10.2 %convolution_bitcast_fusion = f32[2,32,64,768]{3,2,0,1:T(8,128)} fusion(bf16[32,2,64,512]{3,2,1,0:T(8,128)(2,1)} %bitcast.36, bf16[512,768,1,1]{1,0,3,2:T(8,128)(2,1)S(1)} %bitcast.39), kind=kOutput, calls=%fused_computation.5 | convolution fusion | flops 3221225472 | bytes 17563648 | tf_op jit(solution)/shard_map/dot_general | solution.py:69
  151.9 10.5 %copy.11 = f32[2,32,64,768]{3,2,1,0:T(8,128)} copy(f32[2,32,64,768]{3,2,0,1:T(8,128)} %convolution_bitcast_fusion) | data formatting | bytes 25165824 | tf_op jit(solution)/shard_map/transpose | solution.py:43
  162.4 0.0 reduce-scatter.5.cloned.1.call-start
  162.5 27.0 %reduce-scatter.3.cloned.1.call-done = f32[32,64,768]{2,1,0:T(8,128)} async-done(((f32[64,64,768]{2,1,0:T(8,128)}), f32[32,64,768]{2,1,0:T(8,128)}) %reduce-scatter.3.cloned.1.call-update) | async-done | bytes 6291472 | tf_op jit(solution)/shard_map/reduce_scatter | solution.py:44
  189.5 8.0 %fusion.2 = f32[512,768]{1,0:T(8,128)S(1)} fusion(bf16[4096,768]{1,0:T(8,128)(2,1)} %all-gather.3.cloned.1.call-done, f32[512,4096]{1,0:T(8,128)} %get-tuple-element.3, s32[4096]{0:T(1024)S(1)} %iota_add_fusion, f32[]{:T(128)} %bitcast.32, s32[512]{0:T(512)S(1)} %bitcast.41), kind=kOutput, calls=%fused_computation.6 | convolution fusion | flops 3231711232 | bytes 16271364 | tf_op jit(solution)/shard_map/dot_general | solution.py:88
  197.5 60.5 %all_to_all.10 = f32[4,128,768]{2,1,0:T(8,128)S(1)} all-to-all(f32[4,128,768]{2,1,0:T(8,128)S(1)} %bitcast.37), channel_id=1, replica_groups=mesh['group'=4,'member_0'=4,'member_1'=4,'member_2'=2,'member_3'=2] {'gr..., dimensions={0} | all-to-all | bytes 3145728 | tf_op jit(solution)/shard_map/all_to_all | solution.py:35
  258.0 0.1 reduce_sum.47
  258.1 0.2 multiply_reduce_fusion
  258.3 0.9 subtract_divide_fusion
  259.2 146.1 %reduce-scatter.5.cloned.1.call-done = f32[1,64,768]{2,1,0:T(8,128)} async-done(((f32[32,64,768]{2,1,0:T(8,128)}), f32[1,64,768]{2,1,0:T(8,128)}) %reduce-scatter.5.cloned.1.call-update) | async-done | bytes 196624 | tf_op jit(solution)/shard_map/reduce_scatter | solution.py:45
  405.4 1.1 fusion.8
  406.5 1.7 fusion.9
  (11 shorter events, 0.1 us)
Async XLA Ops:
  7.2 117.9 %all-gather.3.cloned.1.call-start = ((), (), s32[]{:S(2)}) async-start(), calls=%async_computation.4 | async-start | bytes 6389760 | tf_op jit(solution)/shard_map/all_gather | solution.py:82
  12.9 36.4 %all-to-all-start = ((bf16[4,128,768]{2,1,0:T(8,128)(2,1)}), bf16[4,128,768]{2,1,0:T(8,128)(2,1)S(1)}, u32[]{:S(2)}, u32[]{:S(2)}) async-start(bf16[4,128,768]{2,1,0:T(8,128)(2,1)} %broadcast_in_dim.2), calls=%async_computation | async-start | bytes 1572864 | tf_op jit(solution)/shard_map/all_to_all | solution.py:19
  21.0 168.4 %reduce-scatter.3.cloned.1.call-start = ((), (), s32[]{:S(2)}) async-start(), calls=%async_computation.5 | async-start | bytes 18874368 | tf_op jit(solution)/shard_map/reduce_scatter | solution.py:44
  162.4 242.9 %reduce-scatter.5.cloned.1.call-start = ((), (), s32[]{:S(2)}) async-start(), calls=%async_computation.6 | async-start | bytes 6488064 | tf_op jit(solution)/shard_map/reduce_scatter | solution.py:45
  189.5 68.7 %copy-start = (bf16[128,768]{1,0:T(8,128)(2,1)S(1)}, bf16[128,768]{1,0:T(8,128)(2,1)}, u32[]{:S(2)}) copy-start(bf16[128,768]{1,0:T(8,128)(2,1)} %param.5) | copy-start | bytes 589828
  189.5 215.9 %copy-start.1 = (bf16[64,768]{1,0:T(8,128)(2,1)S(1)}, bf16[64,768]{1,0:T(8,128)(2,1)}, u32[]{:S(2)}) copy-start(bf16[64,768]{1,0:T(8,128)(2,1)} %param.6) | copy-start | bytes 294916
Sparse Core Ops, SparseCore 0:
  10.4 114.5 all-gather.2
  162.5 26.8 reduce-scatter.2
  192.0 213.3 reduce-scatter.4
where the time goes:
time: 415 us
  waiting for transfers between devices  249 us (60%)
  blocking collectives  87.5 us (21%)
  matrix products  28.3 us (7%)
  local copies, waits for them, and re-layouts  18 us (4%)
  between operations  15.1 us (4%)
  other arithmetic  8.8 us (2%)
  starting transfers between devices  8.19 us (2%)
    reduce_scatter x1, waiting for transfers between devices, scatter_pairs(): return lax.psum_scatter(blocks, chips, scatter_dimension=0, tiled=True)[0]  146 us
    all_gather x1, waiting for transfers between devices, shards(): text_rows = lax.all_gather(text_normalized, MEMBER, axis=0, tiled=True)  75.7 us
    all_to_all x1, blocking collectives, sum_at_owner(): blocks = lax.all_to_all(split_up(value, dim, size), axis, 0, 0, tiled=True)  60.5 us
    all_gather x1, blocking collectives, shards(): label_all = lax.all_gather(matching_indices, 'group', axis=0, tiled=True)  27 us
    reduce_scatter x1, waiting for transfers between devices, scatter_pairs(): blocks = lax.psum_scatter(blocks, core, scatter_dimension=0, tiled=True)  27 us
    transpose x1, local copies, waits for them, and re-layouts, scatter_pairs(): blocks = blocks.reshape(*sizes, *inside).swapaxes(0, 1).reshape(-1, *inside)  10.5 us
    dot_general x1, matrix products, column_product(): lax.dot_general(pair_weight, visitor, (((0,), (0,)), ((), ())), preferred...  10.2 us
    dot_general x1, matrix products, pair_coef(): jnp.dot(audio_entries, text_rows.T, preferred_element_type=jnp.float32)  10.1 us
  transfers between devices with their start and end apart: 4, of which 3 were waited for; matrix products, arithmetic and copies ran while one was open for 3% of the time, Pallas kernels for 0%

commit v1 on v0

--- a/solution.py
+++ b/solution.py
@@ -6,6 +6,13 @@
 
 MEMBER = ("member_0", "member_1", "member_2", "member_3")
 GROUP_MEMBER = ("group", "member_0", "member_1", "member_2", "member_3")
+
+
+def all_by_exchange(block, name, along):
+    size = lax.axis_size(name)
+    shards = jnp.stack([block for _ in range(size)])
+    shards = lax.all_to_all(shards, name, split_axis=0, concat_axis=0)
+    return jnp.concatenate(shards, axis=along)
 
 
 def joined_along(blocks, dim):
@@ -82,7 +89,7 @@
     text_rows = lax.all_gather(text_normalized, MEMBER, axis=0, tiled=True)
     width = text_rows.shape[0]
     columns = group_now * width + jnp.arange(width, dtype=jnp.int32)
-    label_all = lax.all_gather(matching_indices, "group", axis=0, tiled=True)
+    label_all = all_by_exchange(matching_indices, "group", 0)
     speech_all = gather_directly(speech_unit, "group", 0)
     pair_weight = pair_coef(speech_all, label_all, text_rows, columns, sharpness_factor, shift)
     speech_part = jnp.dot(pair_weight, text_rows, preferred_element_type=jnp.float32)

time: 415 us -> 416 us (level)
  blocking collectives: 87.5 us -> 60.7 us
  waiting for transfers between devices: 249 us -> 270 us
  starting transfers between devices: 8.19 us -> 14 us
    all_gather x1 -> x0, blocking collectives: 27 us -> none  [shards(): label_all = lax.all_gather(matching_indices, 'group', axis=0, tiled=True)]
    all_to_all x1, waiting for transfers between devices: 0.01 us -> 25.1 us  [copy_for_each(): lax.all_to_all(jnp.broadcast_to(value[None], (size, *value.shape)), axis,...]
    all_to_all x0 -> x1, starting transfers between devices: none -> 8.11 us  [all_by_exchange(): shards = lax.all_to_all(shards, name, split_axis=0, concat_axis=0)]
    all_gather x1, waiting for transfers between devices: 75.7 us -> 69.2 us  [shards(): text_rows = lax.all_gather(text_normalized, MEMBER, axis=0, tiled=True)]
  transfers between devices with their start and end apart: 4 -> 5, of which waited for: 3 -> 5; matrix products, arithmetic and copies ran while one was open for 3% -> 3% of each run, Pallas kernels for 0% -> 0%
where the time goes in v1:
time: 416 us
  waiting for transfers between devices  270 us (65%)
  blocking collectives  60.7 us (15%)
  matrix products  28.4 us (7%)
  local copies, waits for them, and re-layouts  19.2 us (5%)
  between operations  15.1 us (4%)
  starting transfers between devices  14 us (3%)
  other arithmetic  8.8 us (2%)
    reduce_scatter x1, waiting for transfers between devices, scatter_pairs(): return lax.psum_scatter(blocks, chips, scatter_dimension=0, tiled=True)[0]  146 us
    all_gather x1, waiting for transfers between devices, shards(): text_rows = lax.all_gather(text_normalized, MEMBER, axis=0, tiled=True)  69.2 us
    all_to_all x1, blocking collectives, sum_at_owner(): blocks = lax.all_to_all(split_up(value, dim, size), axis, 0, 0, tiled=True)  60.7 us
    reduce_scatter x1, waiting for transfers between devices, scatter_pairs(): blocks = lax.psum_scatter(blocks, core, scatter_dimension=0, tiled=True)  25.7 us
    all_to_all x1, waiting for transfers between devices, copy_for_each(): lax.all_to_all(jnp.broadcast_to(value[None], (size, *value.shape)), axis,...  25.1 us
    transpose x1, local copies, waits for them, and re-layouts, scatter_pairs(): blocks = blocks.reshape(*sizes, *inside).swapaxes(0, 1).reshape(-1, *inside)  10.5 us
    dot_general x1, matrix products, column_product(): lax.dot_general(pair_weight, visitor, (((0,), (0,)), ((), ())), preferred...  10.2 us
    dot_general x1, matrix products, pair_coef(): jnp.dot(audio_entries, text_rows.T, preferred_element_type=jnp.float32)  10.1 us
  transfers between devices with their start and end apart: 5, of which 5 were waited for; matrix products, arithmetic and copies ran while one was open for 3% of the time, Pallas kernels for 0%

profile of v1, /device:TPU:64, one launch (start us, length us, event | category | flops | bytes accessed | tf_op | source)
XLA Modules:
  0.0 415.8 jit_solution(9708500684130878948)
XLA Ops:
  7.2 1.0 fusion.7
  8.2 1.6 fusion.10
  9.9 1.2 stack.2
  11.1 8.1 %all-to-all-start.1 = ((s32[4,1,128]{2,1,0:T(1,128)}), s32[4,1,128]{2,1,0:T(1,128)S(1)}, u32[]{:S(2)}, u32[]{:S(2)}) async-start(s32[4,1,128]{2,1,0:T(1,128)} %stack.2), calls=%async_computation.1 | async-start | bytes 4096 | tf_op jit(solution)/shard_map/all_to_all | solution.py:14
  19.2 1.0 fusion.6
  20.3 1.0 fusion.11
  21.3 3.2 all-to-all-done.1
  24.5 0.9 broadcast_in_dim.2
  25.4 5.8 %all-to-all-start = ((bf16[4,128,768]{2,1,0:T(8,128)(2,1)}), bf16[4,128,768]{2,1,0:T(8,128)(2,1)S(1)}, u32[]{:S(2)}, u32[]{:S(2)}) async-start(bf16[4,128,768]{2,1,0:T(8,128)(2,1)} %broadcast_in_dim.2), calls=%async_computation | async-start | bytes 1572864 | tf_op jit(solution)/shard_map/all_to_all | solution.py:26
  32.6 25.1 %all-to-all-done = bf16[4,128,768]{2,1,0:T(8,128)(2,1)S(1)} async-done(((bf16[4,128,768]{2,1,0:T(8,128)(2,1)}), bf16[4,128,768]{2,1,0:T(8,128)(2,1)S(1)}, u32[]{:S(2)}, u32[]{:S(2)}) %all-to-all-start) | async-done | bytes 786464 | tf_op jit(solution)/shard_map/all_to_all | solution.py:26
  57.7 69.2 %all-gather.2.cloned.1.call-done = bf16[4096,768]{1,0:T(8,128)(2,1)} async-done(((bf16[64,768]{1,0:T(8,128)(2,1)}), bf16[4096,768]{1,0:T(8,128)(2,1)}) %all-gather.2.cloned.1.call-update) | async-done | bytes 6291472 | tf_op jit(solution)/shard_map/all_gather | solution.py:89
  126.9 10.1 %fusion.1 = (bf16[4096,512]{0,1:T(8,128)(2,1)}, f32[512,4096]{1,0:T(8,128)}) fusion(s32[4096]{0:T(1024)S(1)} %iota_add_fusion, f32[]{:T(128)} %bitcast.32, s32[512]{0:T(512)S(1)} %bitcast.39, f32[]{:T(128)} %bitcast.33, bf16[512,768]{1,0:T(8,128)(2,1)S(1)} %bitcast.37, bf16[4096,768]{1,0:T(8,128)(2,1)} %all-gather.2.cloned.1.call-done), kind=kOutput, calls=%fused_computation.2 | convolution fusion | flops 3242196992 | bytes 19679240 | tf_op jit(solution)/shard_map/dot_general | solution.py:68
  137.0 6.5 %copy.8 = bf16[4096,512]{1,0:T(8,128)(2,1)} copy(bf16[4096,512]{0,1:T(8,128)(2,1)} %get-tuple-element.2) | data formatting | bytes 8388608 | tf_op jit(solution)/shard_map/convert_element_type | solution.py:72
  143.5 10.2 %convolution_bitcast_fusion = f32[2,32,64,768]{3,2,0,1:T(8,128)} fusion(bf16[32,2,64,512]{3,2,1,0:T(8,128)(2,1)} %bitcast.35, bf16[512,768,1,1]{1,0,3,2:T(8,128)(2,1)S(1)} %bitcast.38), kind=kOutput, calls=%fused_computation.5 | convolution fusion | flops 3221225472 | bytes 17563648 | tf_op jit(solution)/shard_map/dot_general | solution.py:76
  153.7 10.5 %copy.9 = f32[2,32,64,768]{3,2,1,0:T(8,128)} copy(f32[2,32,64,768]{3,2,0,1:T(8,128)} %convolution_bitcast_fusion) | data formatting | bytes 25165824 | tf_op jit(solution)/shard_map/transpose | solution.py:50
  164.3 25.7 %reduce-scatter.3.cloned.1.call-done = f32[32,64,768]{2,1,0:T(8,128)} async-done(((f32[64,64,768]{2,1,0:T(8,128)}), f32[32,64,768]{2,1,0:T(8,128)}) %reduce-scatter.3.cloned.1.call-update) | async-done | bytes 6291472 | tf_op jit(solution)/shard_map/reduce_scatter | solution.py:51
  190.1 8.0 %fusion.2 = f32[512,768]{1,0:T(8,128)S(1)} fusion(bf16[4096,768]{1,0:T(8,128)(2,1)} %all-gather.2.cloned.1.call-done, f32[512,4096]{1,0:T(8,128)} %get-tuple-element.3, s32[4096]{0:T(1024)S(1)} %iota_add_fusion, f32[]{:T(128)} %bitcast.31, s32[512]{0:T(512)S(1)} %bitcast.40), kind=kOutput, calls=%fused_computation.6 | convolution fusion | flops 3231711232 | bytes 16271364 | tf_op jit(solution)/shard_map/dot_general | solution.py:95
  198.1 60.7 %all_to_all.16 = f32[4,128,768]{2,1,0:T(8,128)S(1)} all-to-all(f32[4,128,768]{2,1,0:T(8,128)S(1)} %bitcast.36), channel_id=1, replica_groups=mesh['group'=4,'member_0'=4,'member_1'=4,'member_2'=2,'member_3'=2] {'gr..., dimensions={0} | all-to-all | bytes 3145728 | tf_op jit(solution)/shard_map/all_to_all | solution.py:42
  258.8 0.1 reduce_sum.47
  259.0 0.2 multiply_reduce_fusion
  259.2 0.9 subtract_divide_fusion
  260.1 146.4 %reduce-scatter.5.cloned.1.call-done = f32[1,64,768]{2,1,0:T(8,128)} async-done(((f32[32,64,768]{2,1,0:T(8,128)}), f32[1,64,768]{2,1,0:T(8,128)}) %reduce-scatter.5.cloned.1.call-update) | async-done | bytes 196624 | tf_op jit(solution)/shard_map/reduce_scatter | solution.py:52
  406.4 1.1 fusion.8
  407.6 1.7 fusion.9
  (13 shorter events, 0.2 us)
Async XLA Ops:
  7.2 119.7 %all-gather.2.cloned.1.call-start = ((), (), s32[]{:S(2)}) async-start(), calls=%async_computation.5 | async-start | bytes 6389760 | tf_op jit(solution)/shard_map/all_gather | solution.py:89
  11.1 13.4 %all-to-all-start.1 = ((s32[4,1,128]{2,1,0:T(1,128)}), s32[4,1,128]{2,1,0:T(1,128)S(1)}, u32[]{:S(2)}, u32[]{:S(2)}) async-start(s32[4,1,128]{2,1,0:T(1,128)} %stack.2), calls=%async_computation.1 | async-start | bytes 4096 | tf_op jit(solution)/shard_map/all_to_all | solution.py:14
  25.4 32.3 %all-to-all-start = ((bf16[4,128,768]{2,1,0:T(8,128)(2,1)}), bf16[4,128,768]{2,1,0:T(8,128)(2,1)S(1)}, u32[]{:S(2)}, u32[]{:S(2)}) async-start(bf16[4,128,768]{2,1,0:T(8,128)(2,1)} %broadcast_in_dim.2), calls=%async_computation | async-start | bytes 1572864 | tf_op jit(solution)/shard_map/all_to_all | solution.py:26
  31.2 158.8 %reduce-scatter.3.cloned.1.call-start = ((), (), s32[]{:S(2)}) async-start(), calls=%async_computation.6 | async-start | bytes 18874368 | tf_op jit(solution)/shard_map/reduce_scatter | solution.py:51
  164.3 242.2 %reduce-scatter.5.cloned.1.call-start = ((), (), s32[]{:S(2)}) async-start(), calls=%async_computation.7 | async-start | bytes 6488064 | tf_op jit(solution)/shard_map/reduce_scatter | solution.py:52
  190.1 68.9 %copy-start = (bf16[128,768]{1,0:T(8,128)(2,1)S(1)}, bf16[128,768]{1,0:T(8,128)(2,1)}, u32[]{:S(2)}) copy-start(bf16[128,768]{1,0:T(8,128)(2,1)} %param.5) | copy-start | bytes 589828
  190.1 216.4 %copy-start.1 = (bf16[64,768]{1,0:T(8,128)(2,1)S(1)}, bf16[64,768]{1,0:T(8,128)(2,1)}, u32[]{:S(2)}) copy-start(bf16[64,768]{1,0:T(8,128)(2,1)} %param.6) | copy-start | bytes 294916
Sparse Core Ops, SparseCore 0:
  10.4 116.4 all-gather.1
  164.4 25.5 reduce-scatter.2
  192.6 213.7 reduce-scatter.4
